TPU v7x, 32 devices: a whole 2x2x4 slice. The times are simulated.
32 devices in a mesh: slab: 2 (over x), gal: 4 (over y, core), qb: 4 (over z).
Axes of the slice: x: 2, y: 2, z: 4, core: 2. Of those that a mesh axis runs over, the one named last changes fastest.
Arguments:
- gallery: bfloat16 [16384, 768], P(('slab', 'gal')), parts along dimension 0, may hold values from -512 to 512
- querybank: bfloat16 [8, 2048, 768], P(('slab', 'qb'), 'gal'), parts along dimension 0, may hold values from -512 to 512
- test_queries: bfloat16 [8, 512, 768], P(('slab', 'qb'), 'gal'), parts along dimension 0, may hold values from -512 to 512
Outputs:
- logprob: float32 [4096, 8192], P(('slab', 'qb'), 'gal'), parts along dimension 0
- normalizer: float32 [16384], P(('slab', 'gal')), parts along dimension 0
There are 2 independent parts, one for each index of `slab`. A program takes and returns all parts, laid end to end along the dimension named above; each array names one. Nothing has to cross between parts.
All inputs are finite; a program needn't handle non-finite values.
Results may differ from a plain program's by a relative error of at most 0.00049.
Values may be sent and summed in bfloat16 or wider, within the bound.
No kernel may reach another device: no remote copies, remote signals or barrier semaphores. Data moves between devices by JAX's collectives and lax.ppermute only.
A program may use at most 64 MiB of HBM per device.

v0:
```python
import math
import jax
import jax.numpy as jnp
from jax import lax
from jax.sharding import PartitionSpec as P

sharpness = 20.0


def unit_rows(values):
    wide = values.astype(jnp.float32)
    scaled = wide * lax.rsqrt(jnp.sum(wide * wide, axis=-1, keepdims=True) + 1e-06)
    return scaled.astype(jnp.bfloat16)


def column_terms(bank_block, gallery_unit):
    scores = lax.dot_general(
        bank_block, gallery_unit, (((1,), (1,)), ((), ())), preferred_element_type=jnp.float32
    )
    return jnp.sum(jnp.exp(sharpness * (scores - 1.0)), axis=0)


def bank_columns(bank_block, gallery_unit):
    rows = bank_block.shape[0]
    height = math.gcd(rows, 512)

    def add_block(index, running):
        piece = lax.dynamic_slice_in_dim(bank_block, index * height, height, 0)
        return running + column_terms(piece, gallery_unit)

    initial = jnp.zeros((gallery_unit.shape[0],), jnp.float32)
    return lax.fori_loop(0, rows // height, add_block, initial)


def per_device(gallery, querybank, test_queries):
    gallery_unit = unit_rows(gallery)
    bank_local = unit_rows(querybank[0])
    test_local = unit_rows(test_queries[0])
    bank_all = lax.all_gather(bank_local, "gal", axis=0, tiled=True)
    column_part = bank_columns(bank_all, gallery_unit)
    test_all = lax.all_gather(test_local, "gal", axis=0, tiled=True)
    column_total = lax.psum(column_part, "qb")
    normalizer = sharpness + jnp.log(column_total)
    bank_count = querybank.shape[1] * lax.axis_size("gal") * lax.axis_size("qb")
    offset = 2.0 * sharpness - math.log(bank_count)
    scores = lax.dot_general(
        test_all, gallery_unit, (((1,), (1,)), ((), ())), preferred_element_type=jnp.float32
    )
    logits = sharpness * scores - normalizer[None, :] - offset
    row_part = jnp.sum(jnp.exp(logits), axis=1)
    row_total = lax.psum(row_part, "gal")
    logprob = logits - jnp.log(row_total)[:, None]
    return (logprob, normalizer)


def solution(mesh):
    placed = (
        P(("slab", "gal"), None),
        P(("slab", "qb"), "gal", None),
        P(("slab", "qb"), "gal", None),
    )
    return jax.shard_map(
        per_device,
        mesh=mesh,
        in_specs=placed,
        out_specs=(P(("slab", "qb"), "gal"), P(("slab", "gal"))),
        check_vma=False,
    )
```

profile of v0, /device:TPU:0, one launch (start us, length us, event | category | flops | bytes accessed | tf_op | source)
XLA Modules:
  0.0 94.0 jit_solution(4073056862240279345)
XLA Ops:
  7.2 0.0 copy-start.1
  7.2 0.0 copy-start
  7.2 0.0 all-gather.2.cloned.1.call-start
  7.2 1.5 %fusion.5 = f32[512]{0:T(512)S(1)} fusion(bf16[1,512,768]{2,1,0:T(8,128)(2,1)} %param.6), kind=kLoop, calls=%fused_computation.13 | loop fusion | flops 1179136 | bytes 788480 | tf_op jit(solution)/shard_map/reduce_sum | solution.py:12
  8.8 2.2 %fusion.6 = bf16[512,768]{1,0:T(8,128)(2,1)} fusion(bf16[1,512,768]{2,1,0:T(8,128)(2,1)} %param.6, f32[512]{0:T(512)S(1)} %add_rsqrt_fusion.1), kind=kLoop, calls=%fused_computation.14 | loop fusion | flops 1179648 | bytes 1574912 | tf_op jit(solution)/shard_map/convert_element_type | solution.py:13
  11.0 0.0 all-gather.2.cloned.1.call-update
  11.0 1.0 %fusion.7 = f32[128]{0:T(128)S(1)} fusion(bf16[1,128,768]{2,1,0:T(8,128)(2,1)} %param.7), kind=kLoop, calls=%fused_computation.17 | loop fusion | flops 294784 | bytes 197120 | tf_op jit(solution)/shard_map/reduce_sum | solution.py:12
  12.1 0.0 copy-done
  12.1 0.7 fusion.2
  12.8 0.0 copy-done.1
  12.8 0.1 fusion.8
  12.9 10.6 %all_gather.6 = bf16[512,768]{1,0:T(8,128)(2,1)} all-gather(bf16[128,768]{1,0:T(8,128)(2,1)S(1)} %fusion.8), channel_id=1, replica_groups=mesh['slab'=2,'gal'=4,'qb'=4] {'gal'}, dimensions={0}, use_global_device_ids=true | all-gather | bytes 983040 | tf_op jit(solution)/shard_map/all_gather | solution.py:41
  23.5 2.3 %fusion.3 = bf16[2048,768]{1,0:T(8,128)(2,1)} fusion(bf16[2048,768]{1,0:T(8,128)(2,1)S(1)} %copy-done, f32[2048]{0:T(1024)S(1)} %add_rsqrt_fusion), kind=kLoop, calls=%fused_computation.7 | loop fusion | flops 4718592 | bytes 6299648 | tf_op jit(solution)/shard_map/convert_element_type | solution.py:13
  25.8 16.6 %all-gather.2.cloned.1.call-done = bf16[2048,768]{1,0:T(8,128)(2,1)} async-done(((bf16[512,768]{1,0:T(8,128)(2,1)}), bf16[2048,768]{1,0:T(8,128)(2,1)}) %all-gather.2.cloned.1.call-update) | async-done | bytes 3145744 | tf_op jit(solution)/shard_map/all_gather | solution.py:39
  42.4 0.0 copy-start.2
  42.4 16.3 %while.16 = (s32[]{:T(128)}, f32[2048]{0:T(1024)S(1)}, bf16[2048,768]{1,0:T(8,128)(2,1)}, bf16[2048,768]{1,0:T(8,128)(2,1)}, s32[]{:T(128)}, /*index=5*/s32[]{:T(128)}, s32[]{:T(128)}, s32[]{:T(128)}) while((s32[]{:T(128)}, f32[2048]{0:T(1024)S(1)}, bf16[2048,768]{1,0:T(8,128)(2,1)}, bf16[2048,768]{1,0:T(8,128)(2,1)}, s32[]{:T(128)}, ...), condition=%wide.region_5.0_spmd.clone, body=%wide.region_3.0_spmd.clone.sunk | while | flops 1613760512 | bytes 3965081 | solution.py:32
  42.4 4.1 %exponential_reduce_fusion.3 = f32[2048]{0:T(1024)S(1)} fusion(bf16[2048,768]{1,0:T(8,128)(2,1)} %get-tuple-element.182, bf16[2048,768]{1,0:T(8,128)(2,1)} %get-tuple-element.181, s32[]{:T(128)S(6)} %select_n.12), kind=kOutput, calls=%fused_computation.clone.1 | convolution fusion | flops 1613756416 | bytes 3940356 | tf_op jit(solution)/shard_map/while/body/eval_jaxpr/dot_general | solution.py:17
  46.5 4.0 %exponential_reduce_fusion.3 = f32[2048]{0:T(1024)S(1)} fusion(bf16[2048,768]{1,0:T(8,128)(2,1)} %get-tuple-element.182, bf16[2048,768]{1,0:T(8,128)(2,1)} %get-tuple-element.181, s32[]{:T(128)S(6)} %select_n.12), kind=kOutput, calls=%fused_computation.clone.1 | convolution fusion | flops 1613756416 | bytes 3940356 | tf_op jit(solution)/shard_map/while/body/eval_jaxpr/dot_general | solution.py:17
  50.6 4.0 %exponential_reduce_fusion.3 = f32[2048]{0:T(1024)S(1)} fusion(bf16[2048,768]{1,0:T(8,128)(2,1)} %get-tuple-element.182, bf16[2048,768]{1,0:T(8,128)(2,1)} %get-tuple-element.181, s32[]{:T(128)S(6)} %select_n.12), kind=kOutput, calls=%fused_computation.clone.1 | convolution fusion | flops 1613756416 | bytes 3940356 | tf_op jit(solution)/shard_map/while/body/eval_jaxpr/dot_general | solution.py:17
  54.6 4.0 %exponential_reduce_fusion.3 = f32[2048]{0:T(1024)S(1)} fusion(bf16[2048,768]{1,0:T(8,128)(2,1)} %get-tuple-element.182, bf16[2048,768]{1,0:T(8,128)(2,1)} %get-tuple-element.181, s32[]{:T(128)S(6)} %select_n.12), kind=kOutput, calls=%fused_computation.clone.1 | convolution fusion | flops 1613756416 | bytes 3940356 | tf_op jit(solution)/shard_map/while/body/eval_jaxpr/dot_general | solution.py:17
  58.7 11.8 %psum.14 = f32[2048]{0:T(1024)S(1)} all-reduce(f32[2048]{0:T(1024)S(1)} %get-tuple-element.112), channel_id=1, replica_groups=mesh['slab'=2,'gal'=4,'qb'=4] {'qb'}, use_global_device_ids=true, to_apply=%region_6.0 | all-reduce | flops 2048 | bytes 16384 | tf_op jit(solution)/shard_map/psum | solution.py:42
  70.5 0.0 copy-done.2
  70.5 0.0 copy-start.3
  70.6 5.9 %exponential_reduce_fusion.1 = (f32[512]{0:T(512)S(1)}, f32[512,2048]{1,0:T(8,128)}) fusion(f32[2048]{0:T(1024)S(1)} %log_add_fusion, bf16[512,768]{1,0:T(8,128)(2,1)S(1)} %copy-done.2, bf16[2048,768]{1,0:T(8,128)(2,1)} %get-tuple-element.188), kind=kOutput, calls=%fused_computation.8 | convolution fusion | flops 1614806528 | bytes 8136704 | tf_op jit(solution)/shard_map/dot_general | solution.py:46
  76.5 5.9 %psum.15 = f32[512]{0:T(512)S(1)} all-reduce(f32[512]{0:T(512)S(1)} %get-tuple-element.136), channel_id=1, replica_groups=mesh['slab'=2,'gal'=4,'qb'=4] {'gal'}, use_global_device_ids=true, to_apply=%region_8.0 | all-reduce | flops 512 | bytes 4096 | tf_op jit(solution)/shard_map/psum | solution.py:51
  82.4 0.0 copy-done.3
  82.4 4.8 %fusion.4 = f32[512,2048]{1,0:T(8,128)} fusion(f32[512,2048]{1,0:T(8,128)} %get-tuple-element.137, f32[512]{0:T(512)S(1)} %log.7, f32[2048]{0:T(1024)S(1)} %log_add_fusion), kind=kLoop, calls=%fused_computation.10 | loop fusion | flops 4194304 | bytes 8398848 | tf_op jit(solution)/shard_map/sub | solution.py:52
  (10 shorter events, 0.1 us)
Async XLA Ops:
  7.2 5.6 %copy-start.1 = (bf16[1,128,768]{2,1,0:T(8,128)(2,1)S(1)}, bf16[1,128,768]{2,1,0:T(8,128)(2,1)}, u32[]{:S(2)}) copy-start(bf16[1,128,768]{2,1,0:T(8,128)(2,1)} %param.7) | copy-start | bytes 589828
  7.2 4.9 %copy-start = (bf16[2048,768]{1,0:T(8,128)(2,1)S(1)}, bf16[2048,768]{1,0:T(8,128)(2,1)}, u32[]{:S(2)}) copy-start(bf16[2048,768]{1,0:T(8,128)(2,1)} %param.5) | copy-start | bytes 9437188
  7.2 35.2 %all-gather.2.cloned.1.call-start = ((), (), s32[]{:S(2)}) async-start(), calls=%async_computation | async-start | bytes 3932160 | tf_op jit(solution)/shard_map/all_gather | solution.py:39
  42.4 28.2 %copy-start.2 = (bf16[512,768]{1,0:T(8,128)(2,1)S(1)}, bf16[512,768]{1,0:T(8,128)(2,1)}, u32[]{:S(2)}) copy-start(bf16[512,768]{1,0:T(8,128)(2,1)} %all_gather.6) | copy-start | bytes 2359300
  70.5 11.9 %copy-start.3 = (f32[2048]{0:T(1024)}, f32[2048]{0:T(1024)S(1)}, u32[]{:S(2)}) copy-start(f32[2048]{0:T(1024)S(1)} %log_add_fusion) | copy-start | bytes 24580
Sparse Core Ops, SparseCore 0:
  11.1 31.2 all-gather.1
where the time goes:
time: 94.4 us; the launch traced here: 94 us
  blocking collectives  28.3 us (30%)
  matrix products  22.1 us (23%)
  waiting for transfers between devices  16.6 us (18%)
  between operations  14.1 us (15%)
  other arithmetic  12.7 us (13%)
    all_gather x1, waiting for transfers between devices, per_device(): bank_all = lax.all_gather(bank_local, 'gal', axis=0, tiled=True)  16.6 us
    dot_general x4, matrix products, column_terms(): lax.dot_general(bank_block, gallery_unit, (((1,), (1,)), ((), ())), prefe...  16.1 us
    psum x1, blocking collectives, per_device(): column_total = lax.psum(column_part, 'qb')  11.8 us
    all_gather x1, blocking collectives, per_device(): test_all = lax.all_gather(test_local, 'gal', axis=0, tiled=True)  10.6 us
    dot_general x1, matrix products, per_device(): lax.dot_general(test_all, gallery_unit, (((1,), (1,)), ((), ())), preferr...  5.95 us
    psum x1, blocking collectives, per_device(): row_total = lax.psum(row_part, 'gal')  5.9 us
    sub x1, other arithmetic, per_device(): logprob = logits - jnp.log(row_total)[:, None]  4.79 us
    convert_element_type x3, other arithmetic, unit_rows(): return scaled.astype(jnp.bfloat16)  4.59 us
  transfers between devices with their start and end apart: 1, of which 1 were waited for; matrix products, arithmetic and copies ran while one was open for 4% of the time, Pallas kernels for 0%

commit v1 on v0

--- a/solution.py
+++ b/solution.py
@@ -1,3 +1,4 @@
+import functools
 import math
 import jax
 import jax.numpy as jnp
@@ -5,6 +6,25 @@
 from jax.sharding import PartitionSpec as P
 
 sharpness = 20.0
+
+
+def area_pair(q_in, chip_axis):
+    total_devices = jax.lax.axis_size(chip_axis)
+    all_rows = [(kk, (kk + 1) % total_devices) for kk in range(total_devices)]
+
+    def view_ports(w_next):
+        if len(w_next) == total_devices:
+            return w_next
+        a_now = jax.lax.ppermute(w_next[0], chip_axis, all_rows)
+        return view_ports([a_now, *w_next])
+
+    moved = view_ports([q_in])
+    everything = jnp.concatenate(moved, axis=0)
+    seen_now = jax.lax.axis_index(chip_axis)
+    return jnp.roll(everything, (seen_now + 1) * q_in.shape[0], axis=0)
+
+
+state_bench = functools.partial(area_pair, chip_axis="gal")
 
 
 def unit_rows(values):
@@ -38,7 +58,7 @@
     test_local = unit_rows(test_queries[0])
     bank_all = lax.all_gather(bank_local, "gal", axis=0, tiled=True)
     column_part = bank_columns(bank_all, gallery_unit)
-    test_all = lax.all_gather(test_local, "gal", axis=0, tiled=True)
+    test_all = state_bench(test_local)
     column_total = lax.psum(column_part, "qb")
     normalizer = sharpness + jnp.log(column_total)
     bank_count = querybank.shape[1] * lax.axis_size("gal") * lax.axis_size("qb")

time: 94.4 us -> 91.5 us (0.969)
  blocking collectives: 28.3 us -> 17.5 us
  local copies, waits for them, and re-layouts: 0.03 us -> 7.84 us
  matrix products: 22.1 us -> 17.2 us
  waiting for transfers between devices: 16.6 us -> 20.4 us
    ppermute x0 -> x3, waiting for transfers between devices: none -> 17.2 us  [view_ports(): a_now = jax.lax.ppermute(w_next[0], chip_axis, all_rows)]
    all_gather x1, waiting for transfers between devices: 16.6 us -> 3.19 us  [per_device(): bank_all = lax.all_gather(bank_local, 'gal', axis=0, tiled=True)]
    all_gather x1 -> x0, blocking collectives: 10.6 us -> none  [per_device(): test_all = lax.all_gather(test_local, 'gal', axis=0, tiled=True)]
    unnamed x8 -> x14, local copies, waits for them, and re-layouts: 0.02 us -> 7.83 us
    dot_general x4, matrix products: 16.1 us -> 12 us  [column_terms(): lax.dot_general(bank_block, gallery_unit, (((1,), (1,)), ((), ())), prefe...]
  transfers between devices with their start and end apart: 1 -> 4, of which waited for: 1 -> 4; matrix products, arithmetic and copies ran while one was open for 4% -> 14% of each run, Pallas kernels for 0% -> 0%
where the time goes in v1:
time: 91.5 us; the launch traced here: 91 us
  waiting for transfers between devices  20.4 us (22%)
  blocking collectives  17.5 us (19%)
  matrix products  17.2 us (19%)
  between operations  14.1 us (15%)
  other arithmetic  13.3 us (15%)
  local copies, waits for them, and re-layouts  7.84 us (9%)
    ppermute x3, waiting for transfers between devices, view_ports(): a_now = jax.lax.ppermute(w_next[0], chip_axis, all_rows)  17.2 us
    dot_general x4, matrix products, column_terms(): lax.dot_general(bank_block, gallery_unit, (((1,), (1,)), ((), ())), prefe...  12 us
    psum x1, blocking collectives, per_device(): column_total = lax.psum(column_part, 'qb')  11.9 us
    unnamed x14, local copies, waits for them, and re-layouts  7.83 us
    psum x1, blocking collectives, per_device(): row_total = lax.psum(row_part, 'gal')  5.63 us
    dot_general x1, matrix products, per_device(): lax.dot_general(test_all, gallery_unit, (((1,), (1,)), ((), ())), preferr...  5.17 us
    sub x1, other arithmetic, per_device(): logprob = logits - jnp.log(row_total)[:, None]  4.79 us
    convert_element_type x3, other arithmetic, unit_rows(): return scaled.astype(jnp.bfloat16)  4.57 us
  transfers between devices with their start and end apart: 4, of which 4 were waited for; matrix products, arithmetic and copies ran while one was open for 14% of the time, Pallas kernels for 0%

profile of v1, /device:TPU:0, one launch (start us, length us, event | category | flops | bytes accessed | tf_op | source)
XLA Modules:
  0.0 91.0 jit_solution(16841833736631148777)
XLA Ops:
  7.2 0.0 all-gather.2.cloned.1.call-start
  7.2 1.5 %fusion.5 = f32[512]{0:T(512)S(1)} fusion(bf16[1,512,768]{2,1,0:T(8,128)(2,1)} %param.6), kind=kLoop, calls=%fused_computation.13 | loop fusion | flops 1179136 | bytes 788480 | tf_op jit(solution)/shard_map/reduce_sum | solution.py:32
  8.8 2.2 %fusion.6 = bf16[512,768]{1,0:T(8,128)(2,1)} fusion(bf16[1,512,768]{2,1,0:T(8,128)(2,1)} %param.6, f32[512]{0:T(512)S(1)} %add_rsqrt_fusion.1), kind=kLoop, calls=%fused_computation.14 | loop fusion | flops 1179648 | bytes 1574912 | tf_op jit(solution)/shard_map/convert_element_type | solution.py:33
  11.0 0.0 all-gather.2.cloned.1.call-update
  11.0 0.1 fusion.9
  11.1 0.1 fusion.10
  11.3 0.5 collective-permute-start
  11.8 0.7 fusion.2
  12.5 4.6 %collective-permute-done = bf16[128,768]{1,0:T(8,128)(2,1)S(1)} collective-permute-done((bf16[128,768]{1,0:T(8,128)(2,1)S(1)}, bf16[128,768]{1,0:T(8,128)(2,1)S(1)}, u32[]{:S(2)}, u32[]{:S(2)}) %collective-permute-start) | collective-permute-done | bytes 196640 | tf_op jit(solution)/shard_map/ppermute | solution.py:18
  17.1 0.0 collective-permute-start.1
  17.1 5.2 %collective-permute-done.1 = bf16[128,768]{1,0:T(8,128)(2,1)} collective-permute-done((bf16[128,768]{1,0:T(8,128)(2,1)S(1)}, bf16[128,768]{1,0:T(8,128)(2,1)}, u32[]{:S(2)}, u32[]{:S(2)}) %collective-permute-start.1) | collective-permute-done | bytes 196640 | tf_op jit(solution)/shard_map/ppermute | solution.py:18
  22.3 2.2 %fusion.3 = bf16[2048,768]{1,0:T(8,128)(2,1)} fusion(bf16[2048,768]{1,0:T(8,128)(2,1)S(1)} %copy-done, f32[2048]{0:T(1024)S(1)} %add_rsqrt_fusion), kind=kLoop, calls=%fused_computation.7 | loop fusion | flops 4718592 | bytes 6299648 | tf_op jit(solution)/shard_map/convert_element_type | solution.py:33
  24.5 7.4 %collective-permute-done.2 = bf16[128,768]{1,0:T(8,128)(2,1)} collective-permute-done((bf16[128,768]{1,0:T(8,128)(2,1)}, bf16[128,768]{1,0:T(8,128)(2,1)}, u32[]{:S(2)}, u32[]{:S(2)}) %collective-permute-start.2) | collective-permute-done | bytes 196640 | tf_op jit(solution)/shard_map/ppermute | solution.py:18
  31.9 1.6 %constant_dynamic-update-slice_fusion.7 = bf16[1024,768]{1,0:T(8,128)(2,1)} fusion(bf16[128,768]{1,0:T(8,128)(2,1)} %collective-permute-done.2), kind=kLoop, calls=%fused_computation.28 | loop fusion | bytes 393216
  33.6 1.6 %constant_dynamic-update-slice_fusion.6 = bf16[1024,768]{1,0:T(8,128)(2,1)} fusion(bf16[1024,768]{1,0:T(8,128)(2,1)} %constant_dynamic-update-slice_fusion.7, bf16[128,768]{1,0:T(8,128)(2,1)} %collective-permute-done.1), kind=kLoop, calls=%fused_computation.27 | loop fusion | bytes 393216
  35.2 0.7 constant_dynamic-update-slice_fusion.5
  35.9 0.8 constant_dynamic-update-slice_fusion.4
  36.6 1.6 %constant_dynamic-update-slice_fusion.3 = bf16[1024,768]{1,0:T(8,128)(2,1)} fusion(bf16[1024,768]{1,0:T(8,128)(2,1)} %constant_dynamic-update-slice_fusion.4, bf16[128,768]{1,0:T(8,128)(2,1)} %collective-permute-done.2), kind=kLoop, calls=%fused_computation.24 | loop fusion | bytes 393216
  38.2 1.6 %constant_dynamic-update-slice_fusion.2 = bf16[1024,768]{1,0:T(8,128)(2,1)} fusion(bf16[1024,768]{1,0:T(8,128)(2,1)} %constant_dynamic-update-slice_fusion.3, bf16[128,768]{1,0:T(8,128)(2,1)} %collective-permute-done.1), kind=kLoop, calls=%fused_computation.23 | loop fusion | bytes 393216
  39.8 0.7 constant_dynamic-update-slice_fusion.1
  40.5 0.8 constant_dynamic-update-slice_fusion
  41.3 3.2 %all-gather.2.cloned.1.call-done = bf16[2048,768]{1,0:T(8,128)(2,1)} async-done(((bf16[512,768]{1,0:T(8,128)(2,1)}), bf16[2048,768]{1,0:T(8,128)(2,1)}) %all-gather.2.cloned.1.call-update) | async-done | bytes 3145744 | tf_op jit(solution)/shard_map/all_gather | solution.py:59
  44.5 12.2 %while.16 = (s32[]{:T(128)}, f32[2048]{0:T(1024)S(1)}, bf16[2048,768]{1,0:T(8,128)(2,1)}, bf16[2048,768]{1,0:T(8,128)(2,1)S(1)}, s32[]{:T(128)}, /*index=5*/s32[]{:T(128)}, s32[]{:T(128)}, s32[]{:T(128)}) while((s32[]{:T(128)}, f32[2048]{0:T(1024)S(1)}, bf16[2048,768]{1,0:T(8,128)(2,1)}, bf16[2048,768]{1,0:T(8,128)(2,1)S(1)}, ...), condition=%wide.region_5.0_spmd.clone, body=%wide.region_3.0_spmd.clone.sunk | while | flops 1613760512 | bytes 3965081 | solution.py:52
  44.5 3.0 %exponential_reduce_fusion.3 = f32[2048]{0:T(1024)S(1)} fusion(bf16[2048,768]{1,0:T(8,128)(2,1)S(1)} %get-tuple-element.182, bf16[2048,768]{1,0:T(8,128)(2,1)} %get-tuple-element.181, s32[]{:T(128)S(6)} %select_n.27), kind=kOutput, calls=%fused_computation.clone.1 | convolution fusion | flops 1613756416 | bytes 3940356 | tf_op jit(solution)/shard_map/while/body/eval_jaxpr/dot_general | solution.py:37
  47.6 3.0 %exponential_reduce_fusion.3 = f32[2048]{0:T(1024)S(1)} fusion(bf16[2048,768]{1,0:T(8,128)(2,1)S(1)} %get-tuple-element.182, bf16[2048,768]{1,0:T(8,128)(2,1)} %get-tuple-element.181, s32[]{:T(128)S(6)} %select_n.27), kind=kOutput, calls=%fused_computation.clone.1 | convolution fusion | flops 1613756416 | bytes 3940356 | tf_op jit(solution)/shard_map/while/body/eval_jaxpr/dot_general | solution.py:37
  50.6 3.0 %exponential_reduce_fusion.3 = f32[2048]{0:T(1024)S(1)} fusion(bf16[2048,768]{1,0:T(8,128)(2,1)S(1)} %get-tuple-element.182, bf16[2048,768]{1,0:T(8,128)(2,1)} %get-tuple-element.181, s32[]{:T(128)S(6)} %select_n.27), kind=kOutput, calls=%fused_computation.clone.1 | convolution fusion | flops 1613756416 | bytes 3940356 | tf_op jit(solution)/shard_map/while/body/eval_jaxpr/dot_general | solution.py:37
  53.7 3.0 %exponential_reduce_fusion.3 = f32[2048]{0:T(1024)S(1)} fusion(bf16[2048,768]{1,0:T(8,128)(2,1)S(1)} %get-tuple-element.182, bf16[2048,768]{1,0:T(8,128)(2,1)} %get-tuple-element.181, s32[]{:T(128)S(6)} %select_n.27), kind=kOutput, calls=%fused_computation.clone.1 | convolution fusion | flops 1613756416 | bytes 3940356 | tf_op jit(solution)/shard_map/while/body/eval_jaxpr/dot_general | solution.py:37
  56.7 11.9 %psum.14 = f32[2048]{0:T(1024)S(1)} all-reduce(f32[2048]{0:T(1024)S(1)} %get-tuple-element.112), channel_id=1, replica_groups=mesh['slab'=2,'gal'=4,'qb'=4] {'qb'}, use_global_device_ids=true, to_apply=%region_6.7 | all-reduce | flops 2048 | bytes 16384 | tf_op jit(solution)/shard_map/psum | solution.py:62
  68.6 0.0 copy-start.3
  68.6 5.2 %exponential_reduce_fusion.1 = (f32[512]{0:T(512)S(1)}, f32[512,2048]{1,0:T(8,128)}) fusion(f32[2048]{0:T(1024)S(1)} %log_add_fusion, bf16[2048,768]{1,0:T(8,128)(2,1)S(1)} %get-tuple-element.188, bf16[1024,768]{1,0:T(8,128)(2,1)} %constant_dynamic-update-slice_fusion, s32[]{:T(128)S(6)} %select_n.24), kind=kOutput, calls=%fused_computation.8 | convolution fusion | flops 1614806528 | bytes 8136708 | tf_op jit(solution)/shard_map/dot_general | solution.py:66
  73.8 5.6 %psum.15 = f32[512]{0:T(512)S(1)} all-reduce(f32[512]{0:T(512)S(1)} %get-tuple-element.136), channel_id=1, replica_groups=mesh['slab'=2,'gal'=4,'qb'=4] {'gal'}, use_global_device_ids=true, to_apply=%region_8.9 | all-reduce | flops 512 | bytes 4096 | tf_op jit(solution)/shard_map/psum | solution.py:71
  79.4 4.8 %fusion.4 = f32[512,2048]{1,0:T(8,128)} fusion(f32[512,2048]{1,0:T(8,128)} %get-tuple-element.137, f32[512]{0:T(512)S(1)} %log.7, f32[2048]{0:T(1024)S(1)} %log_add_fusion), kind=kLoop, calls=%fused_computation.10 | loop fusion | flops 4194304 | bytes 8398848 | tf_op jit(solution)/shard_map/sub | solution.py:72
  (18 shorter events, 0.1 us)
Async XLA Ops:
  7.2 3.8 %copy-start.2 = (bf16[1,128,768]{2,1,0:T(8,128)(2,1)S(1)}, bf16[1,128,768]{2,1,0:T(8,128)(2,1)}, u32[]{:S(2)}) copy-start(bf16[1,128,768]{2,1,0:T(8,128)(2,1)} %param.7) | copy-start | bytes 589828
  7.2 4.6 %copy-start = (bf16[2048,768]{1,0:T(8,128)(2,1)S(1)}, bf16[2048,768]{1,0:T(8,128)(2,1)}, u32[]{:S(2)}) copy-start(bf16[2048,768]{1,0:T(8,128)(2,1)} %param.5) | copy-start | bytes 9437188
  7.2 37.3 %all-gather.2.cloned.1.call-start = ((), (), s32[]{:S(2)}) async-start(), calls=%async_computation | async-start | bytes 3932160 | tf_op jit(solution)/shard_map/all_gather | solution.py:59
  11.3 5.8 %collective-permute-start = (bf16[128,768]{1,0:T(8,128)(2,1)S(1)}, bf16[128,768]{1,0:T(8,128)(2,1)S(1)}, u32[]{:S(2)}, u32[]{:S(2)}) collective-permute-start(bf16[128,768]{1,0:T(8,128)(2,1)S(1)} %fusion.10), channel_id=1, source_target_pairs={{0,4},{4,8},{8,12},{12,0},{1,5},{5,9},{9,13},{13,1},{2,6},{6,10},{... | collective-permute-start | bytes 589832 | tf_op jit(solution)/shard_map/ppermute | solution.py:18
  17.1 5.2 %collective-permute-start.1 = (bf16[128,768]{1,0:T(8,128)(2,1)S(1)}, bf16[128,768]{1,0:T(8,128)(2,1)}, u32[]{:S(2)}, u32[]{:S(2)}) collective-permute-start(bf16[128,768]{1,0:T(8,128)(2,1)S(1)} %collective-permute-done), channel_id=1, source_target_pairs={{0,4},{4,8},{8,12},{12,0},{1,5},{5,9},{9,13},{13,1},{2,6},{6,10},{... | collective-permute-start | bytes 589832 | tf_op jit(solution)/shard_map/ppermute | solution.py:18
  22.3 9.6 %collective-permute-start.2 = (bf16[128,768]{1,0:T(8,128)(2,1)}, bf16[128,768]{1,0:T(8,128)(2,1)}, u32[]{:S(2)}, u32[]{:S(2)}) collective-permute-start(bf16[128,768]{1,0:T(8,128)(2,1)} %collective-permute-done.1), channel_id=1, source_target_pairs={{0,4},{4,8},{8,12},{12,0},{1,5},{5,9},{9,13},{13,1},{2,6},{6,10},{... | collective-permute-start | bytes 589832 | tf_op jit(solution)/shard_map/ppermute | solution.py:18
  24.5 20.0 %copy-start.1 = (bf16[2048,768]{1,0:T(8,128)(2,1)S(1)}, bf16[2048,768]{1,0:T(8,128)(2,1)}, u32[]{:S(2)}) copy-start(bf16[2048,768]{1,0:T(8,128)(2,1)} %fusion.3) | copy-start | bytes 9437188
  68.6 10.8 %copy-start.3 = (f32[2048]{0:T(1024)}, f32[2048]{0:T(1024)S(1)}, u32[]{:S(2)}) copy-start(f32[2048]{0:T(1024)S(1)} %log_add_fusion) | copy-start | bytes 24580
Sparse Core Ops, SparseCore 0:
  11.1 33.3 all-gather.1
